TPU v7x, 32 devices: a whole 2x2x4 slice. The times are simulated.
32 devices in a mesh: wide: 16 (over z, y, x), narrow: 2 (over core).
Axes of the slice: x: 2, y: 2, z: 4, core: 2. Of those that a mesh axis runs over, the one named last changes fastest.
Arguments:
- x_trial: float32 [2, 512, 512], P(None, 'wide', 'narrow'), may hold values from -6 to 6
- psi_orb: float32 [512, 16384], P('narrow', 'wide'), may hold values from -0.046875 to 0.046875
- phi_orb: float32 [512, 16384], P('wide', 'narrow'), may hold values from -0.046875 to 0.046875
- screened: float32 [16384, 16384], P('wide', 'narrow'), may hold values from -192 to 192
- eps_val: float32 [512], P('wide'), may hold values from -1 to -0.1
- eps_cond: float32 [512], P('narrow'), may hold values from 0.1 to 1
Outputs:
- applied: float32 [2, 512, 512], P(None, 'wide', 'narrow')
All inputs are finite; a program needn't handle non-finite values.
Results may differ from a plain program's by a relative error of at most 0.00011.
Values sent between devices are 32-bit elements; how exact they have to be, the bound alone decides.
A program may use at most 192 MiB of HBM per device.

v0:
```python
import jax
import jax.numpy as jnp
from jax import lax
from jax.sharding import PartitionSpec as P


def local(x_trial, psi_orb, phi_orb, screened, eps_val, eps_cond):
    precise = lax.Precision.HIGHEST
    psi_rows = lax.all_gather(psi_orb, "narrow", axis=0, tiled=True)
    phi_cols = lax.all_gather(phi_orb, "wide", axis=0, tiled=True)
    x_cols = lax.all_gather(x_trial, "narrow", axis=2, tiled=True)
    x_whole = lax.all_gather(x_cols, "wide", axis=1, tiled=True)
    half_map = jnp.einsum("vr,tvc->trc", psi_rows, x_whole, precision=precise)
    pair_tile = jnp.einsum("trc,cs->trs", half_map, phi_cols, precision=precise) * screened[None]
    back_map = jnp.einsum("trs,cs->trc", pair_tile, phi_cols, precision=precise)
    summed = lax.psum_scatter(back_map, "narrow", scatter_dimension=2, tiled=True)
    val_part = jnp.einsum("vr,trc->tvc", psi_rows, summed, precision=precise)
    kernel = lax.psum_scatter(val_part, "wide", scatter_dimension=1, tiled=True)
    energy_gap = eps_cond[None, None, :] - eps_val[None, :, None]
    return kernel + energy_gap * x_trial


def solution(mesh):
    placed = (
        P(None, "wide", "narrow"),
        P("narrow", "wide"),
        P("wide", "narrow"),
        P("wide", "narrow"),
        P("wide"),
        P("narrow"),
    )
    return jax.shard_map(
        local, mesh=mesh, in_specs=placed, out_specs=P(None, "wide", "narrow"), check_vma=False
    )
```

profile of v0, /device:TPU:14, one launch (start us, length us, event | category | flops | bytes accessed | tf_op | source)
XLA Modules:
  0.0 644.1 jit_solution(13201375299929367361)
XLA Ops:
  6.5 0.0 all-gather.6.cloned.1.call-start
  6.5 0.7 all-gather.6.cloned.1.call-update
  7.3 0.0 all-gather.4.cloned.1.call-start
  7.3 3.4 all_gather.12
  10.7 0.0 all-gather.4.cloned.1.call-update
  10.7 0.0 all-gather.8.cloned.1.call-start
  10.8 0.7 all-gather.8.cloned.1.call-update
  11.4 0.0 reduce-scatter.2.cloned.1.call-start
  11.5 9.3 %all-gather.6.cloned.1.call-done = f32[512,1024]{1,0:T(8,128)} async-done(((f32[256,1024]{1,0:T(8,128)}), f32[512,1024]{1,0:T(8,128)}) %all-gather.6.cloned.1.call-update) | async-done | bytes 2097168 | tf_op jit(solution)/shard_map/all_gather | solution.py:9
  20.8 63.1 %all-gather.4.cloned.1.call-done = f32[2,512,512]{2,1,0:T(8,128)} async-done(((f32[2,32,512]{2,1,0:T(8,128)}), f32[2,512,512]{2,1,0:T(8,128)}) %all-gather.4.cloned.1.call-update) | async-done | bytes 2097168 | tf_op jit(solution)/shard_map/all_gather | solution.py:12
  84.0 10.3 %fusion.9 = f32[2,512,1024]{2,1,0:T(8,128)} fusion(f32[2,512,512]{2,1,0:T(8,128)} %all-gather.4.cloned.1.call-done, f32[512,1024]{1,0:T(8,128)} %all-gather.6.cloned.1.call-done), kind=kOutput, calls=%fused_computation.9 | convolution fusion | flops 6442450944 | bytes 8388608 | tf_op jit(solution)/shard_map/vr,tvc->trc/dot_general | solution.py:13
  94.2 180.4 %all-gather.8.cloned.1.call-done = f32[512,8192]{1,0:T(8,128)} async-done(((f32[32,8192]{1,0:T(8,128)}), f32[512,8192]{1,0:T(8,128)}) %all-gather.8.cloned.1.call-update) | async-done | bytes 16777232 | tf_op jit(solution)/shard_map/all_gather | solution.py:10
  274.7 112.7 %fusion.4 = f32[2,1024,8192]{2,1,0:T(8,128)} fusion(f32[512,8192]{1,0:T(8,128)} %all-gather.8.cloned.1.call-done, f32[2,512,1024]{2,1,0:T(8,128)} %fusion.9), kind=kOutput, calls=%fused_computation.4 | convolution fusion | flops 103079215104 | bytes 88080384 | tf_op jit(solution)/shard_map/trc,cs->trs/dot_general | solution.py:14
  387.4 112.9 %fusion = f32[2,1024,512]{2,1,0:T(8,128)} fusion(f32[2,1024,8192]{2,1,0:T(8,128)} %fusion.4, f32[1024,8192]{1,0:T(8,128)} %param.9, f32[512,8192]{1,0:T(8,128)} %all-gather.8.cloned.1.call-done), kind=kOutput, calls=%fused_computation | convolution fusion | flops 103095992320 | bytes 121634816 | tf_op jit(solution)/shard_map/trs,cs->trc/dot_general | solution.py:15
  500.3 0.0 reduce-scatter.2.cloned.1.call-update
  500.3 0.0 copy-start.4
  500.3 0.0 copy-start.2
  500.3 0.0 copy-start.3
  500.4 0.0 copy-start.1
  500.4 0.3 all-reduce.3.cloned.1.call-start
  500.7 13.0 %reduce-scatter.2.cloned.1.call-done = f32[2,1024,256]{2,1,0:T(8,128)} async-done(((f32[2,1024,512]{2,1,0:T(8,128)}), f32[2,1024,256]{2,1,0:T(8,128)}) %reduce-scatter.2.cloned.1.call-update) | async-done | bytes 2097168 | tf_op jit(solution)/shard_map/reduce_scatter | solution.py:16
  513.7 0.0 copy-done
  513.7 8.3 %fusion.11 = f32[2,512,256]{1,2,0:T(8,128)S(1)} fusion(f32[2,1024,256]{2,1,0:T(8,128)} %reduce-scatter.2.cloned.1.call-done, f32[512,1024]{1,0:T(8,128)S(1)} %copy-done), kind=kOutput, calls=%fused_computation.11 | convolution fusion | flops 3221225472 | bytes 5242880 | tf_op jit(solution)/shard_map/vr,trc->tvc/dot_general | solution.py:17
  522.0 1.3 copy.14
  523.3 0.0 all-reduce.3.cloned.1.call-update
  523.3 0.0 copy-done.4
  523.3 0.6 dynamic-slice
  524.5 0.0 copy-done.2
  524.6 0.1 broadcast_subtract_fusion
  524.6 111.5 %all-reduce.3.cloned.1.call-done = f32[2,512,256]{2,0,1:T(2,128)} async-done(((f32[2,512,256]{2,0,1:T(2,128)}), f32[2,512,256]{2,0,1:T(2,128)}) %all-reduce.3.cloned.1.call-update) | async-done | bytes 1048592
  636.1 0.8 constant_dynamic-slice_fusion
  636.9 0.6 copy_add_fusion
  (3 shorter events, 0.0 us)
Async XLA Ops:
  6.5 14.3 %all-gather.6.cloned.1.call-start = ((), (), s32[]{:S(2)}) async-start(), calls=%async_computation.2 | async-start | bytes 3145728 | tf_op jit(solution)/shard_map/all_gather | solution.py:9
  7.3 76.7 %all-gather.4.cloned.1.call-start = ((), (), s32[]{:S(2)}) async-start(), calls=%async_computation.1 | async-start | bytes 2228224 | tf_op jit(solution)/shard_map/all_gather | solution.py:12
  10.7 263.9 %all-gather.8.cloned.1.call-start = ((), (), s32[]{:S(2)}) async-start(), calls=%async_computation.3 | async-start | bytes 17825792 | tf_op jit(solution)/shard_map/all_gather | solution.py:10
  11.4 502.2 %reduce-scatter.2.cloned.1.call-start = ((), (), s32[]{:S(2)}) async-start(), calls=%async_computation.4 | async-start | bytes 6291456 | tf_op jit(solution)/shard_map/reduce_scatter | solution.py:16
  500.3 13.4 %copy-start = (f32[512,1024]{1,0:T(8,128)S(1)}, f32[512,1024]{1,0:T(8,128)}, u32[]{:S(2)}) copy-start(f32[512,1024]{1,0:T(8,128)} %all-gather.6.cloned.1.call-done) | copy-start | bytes 6291460
  500.3 23.0 %copy-start.4 = (u32[32]{0:T(128)S(1)}, u32[32]{0:T(128)}, u32[]{:S(2)}) copy-start(u32[32]{0:T(128)} %constant.2) | copy-start | bytes 388
  500.3 24.2 %copy-start.2 = (f32[256]{0:T(256)S(1)}, f32[256]{0:T(256)}, u32[]{:S(2)}) copy-start(f32[256]{0:T(256)} %param.11) | copy-start | bytes 3076
  500.3 24.2 %copy-start.3 = (f32[32]{0:T(128)S(1)}, f32[32]{0:T(128)}, u32[]{:S(2)}) copy-start(f32[32]{0:T(128)} %param.10) | copy-start | bytes 388
  500.4 136.6 %copy-start.1 = (f32[2,32,256]{2,1,0:T(8,128)S(1)}, f32[2,32,256]{2,1,0:T(8,128)}, u32[]{:S(2)}) copy-start(f32[2,32,256]{2,1,0:T(8,128)} %param.6) | copy-start | bytes 196612
  500.4 135.7 %all-reduce.3.cloned.1.call-start = ((), (), s32[]{:S(2)}) async-start(), calls=%async_computation.5 | async-start | bytes 2097152
Sparse Core Ops, SparseCore 0:
  8.9 11.9 all-gather.5
  23.6 60.3 all-gather.3
  86.7 187.8 all-gather.7
  500.4 13.1 reduce-scatter.1
  523.4 112.6 all-reduce.2
where the time goes:
time: 647 us; the launch traced here: 644 us
  waiting for transfers between devices  379 us (59%)
  matrix products  244 us (38%)
  between operations  13.9 us (2%)
    all_gather x1, waiting for transfers between devices, local(): phi_cols = lax.all_gather(phi_orb, 'wide', axis=0, tiled=True)  180 us
    dot_general x1, matrix products, local(): back_map = jnp.einsum('trs,cs->trc', pair_tile, phi_cols, precision=precise)  113 us
    unnamed x6, waiting for transfers between devices  113 us
    dot_general x1, matrix products, local(): jnp.einsum('trc,cs->trs', half_map, phi_cols, precision=precise)  113 us
    all_gather x1, waiting for transfers between devices, local(): x_whole = lax.all_gather(x_cols, 'wide', axis=1, tiled=True)  63.1 us
    reduce_scatter x1, waiting for transfers between devices, local(): lax.psum_scatter(back_map, 'narrow', scatter_dimension=2, tiled=True)  13 us
  transfers between devices with their start and end apart: 5, of which 5 were waited for; matrix products, arithmetic and copies ran while one was open for 2% of the time, Pallas kernels for 0%

commit v1 on v0

v1 whole, which is shorter than its diff:
```python
import functools
import math

import jax
import jax.numpy as jnp
from jax import lax
from jax.experimental import pallas as pl
from jax.experimental.pallas import tpu as pltpu
from jax.sharding import PartitionSpec as P

MESH = pl.DeviceIdType.MESH
VM = pl.BlockSpec(memory_space=pltpu.VMEM)
CHUNKS = (2, 2, 2, 1, 1)


def spread_kernel(n, m, x_ref, psi_ref, xs_ref, psis_ref, xs_sem, xr_sem, fs_sem, fr_sem, ps_sem, pr_sem, own_sem):
    w = lax.axis_index("wide")
    c = lax.axis_index("narrow")

    def psi_copy(slot, peer, k):
        return pltpu.make_async_remote_copy(
            src_ref=psi_ref, dst_ref=psis_ref.at[slot], send_sem=ps_sem.at[k], recv_sem=pr_sem.at[slot],
            device_id=(w, peer), device_id_type=MESH)

    def x_copy(slot, peer, k):
        return pltpu.make_async_remote_copy(
            src_ref=x_ref, dst_ref=xs_ref.at[c, slot], send_sem=xs_sem.at[k], recv_sem=xr_sem.at[slot],
            device_id=(peer, c), device_id_type=MESH)

    def forward(src, slot_c, slot, peer, k):
        return pltpu.make_async_remote_copy(
            src_ref=src, dst_ref=xs_ref.at[slot_c, slot], send_sem=fs_sem.at[k, slot],
            recv_sem=fr_sem.at[slot_c, slot], device_id=(w, peer), device_id_type=MESH)

    @pl.loop(1, n)
    def _(i):
        x_copy(w, lax.rem(w + i, n), i).start()

    @pl.loop(1, m)
    def _(j):
        forward(x_ref, c, w, lax.rem(c + j, m), j).start()
        psi_copy(c, lax.rem(c + j, m), j).start()

    own_x = pltpu.make_async_copy(x_ref, xs_ref.at[c, w], own_sem.at[0])
    own_psi = pltpu.make_async_copy(psi_ref, psis_ref.at[c], own_sem.at[1])
    own_x.start()
    own_psi.start()

    @pl.loop(1, n)
    def _(i):
        src = lax.rem(w + n - i, n)
        x_copy(src, w, i).wait_recv()

        @pl.loop(1, m)
        def _(j):
            forward(xs_ref.at[c, src], c, src, lax.rem(c + j, m), j).start()

    own_x.wait()
    own_psi.wait()

    @pl.loop(1, m)
    def _(j):
        other = lax.rem(c + m - j, m)
        psi_copy(other, c, j).wait_recv()
        psi_copy(c, c, j).wait_send()

        @pl.loop(0, n)
        def _(i):
            forward(x_ref, other, i, c, j).wait_recv()
            forward(x_ref, c, i, c, j).wait_send()

    @pl.loop(1, n)
    def _(i):
        x_copy(w, w, i).wait_send()


def spread(n, m, x_trial, psi_orb):
    return pl.pallas_call(
        functools.partial(spread_kernel, n, m),
        out_shape=(
            jax.ShapeDtypeStruct((m, n) + x_trial.shape, jnp.float32),
            jax.ShapeDtypeStruct((m,) + psi_orb.shape, jnp.float32),
        ),
        in_specs=[VM, VM],
        out_specs=(VM, VM),
        scratch_shapes=[
            pltpu.SemaphoreType.DMA((n,)),
            pltpu.SemaphoreType.DMA((n,)),
            pltpu.SemaphoreType.DMA((m, n)),
            pltpu.SemaphoreType.DMA((m, n)),
            pltpu.SemaphoreType.DMA((m,)),
            pltpu.SemaphoreType.DMA((m,)),
            pltpu.SemaphoreType.DMA((2,)),
        ],
        compiler_params=pltpu.CompilerParams(has_side_effects=True),
        name="spread",
    )(x_trial, psi_orb)


def collect_kernel(n, part_ref, out_ref, got, s_sem, r_sem):
    w = lax.axis_index("wide")
    c = lax.axis_index("narrow")

    def copy(block, slot, peer, k):
        return pltpu.make_async_remote_copy(
            src_ref=part_ref.at[block], dst_ref=got.at[slot], send_sem=s_sem.at[k], recv_sem=r_sem.at[slot],
            device_id=(peer, c), device_id_type=MESH)

    @pl.loop(1, n)
    def _(i):
        peer = lax.rem(w + i, n)
        copy(peer, w, peer, i).start()

    out_ref[...] = part_ref[w]

    @pl.loop(1, n)
    def _(i):
        src = lax.rem(w + n - i, n)
        copy(src, src, w, i).wait_recv()
        out_ref[...] += got[src]

    @pl.loop(1, n)
    def _(i):
        copy(w, w, w, i).wait_send()


def collect(n, part):
    return pl.pallas_call(
        functools.partial(collect_kernel, n),
        out_shape=jax.ShapeDtypeStruct(part.shape[1:], jnp.float32),
        in_specs=[VM],
        out_specs=VM,
        scratch_shapes=[
            pltpu.VMEM(part.shape, jnp.float32),
            pltpu.SemaphoreType.DMA((n,)),
            pltpu.SemaphoreType.DMA((n,)),
        ],
        compiler_params=pltpu.CompilerParams(has_side_effects=True),
        name="collect",
    )(part)


def halves(a):
    high = a.astype(jnp.bfloat16)
    return high, (a - high.astype(jnp.float32)).astype(jnp.bfloat16)


def dot3(a, b, dims):
    def one(p, q):
        return lax.dot_general(p, q, (dims, ((), ())), preferred_element_type=jnp.float32)

    return one(a[0], b[0]) + (one(a[0], b[1]) + one(a[1], b[0]))


def tile_kernel(first, rows, half_ref, phi_ref, screened_ref, *refs):
    if first:
        back_ref, high, low = refs
    else:
        sum_ref, back_ref, high, low = refs
    trials, points, _ = half_ref.shape
    steps = points // rows

    @pl.when(pl.program_id(0) == 0)
    def _():
        for t in range(trials):
            @pl.loop(0, steps)
            def _(r):
                at = pl.ds(pl.multiple_of(r * rows, rows), rows)
                high[t, at], low[t, at] = halves(half_ref[t, at])
                back_ref[t, at] = jnp.zeros_like(half_ref[t, at]) if first else sum_ref[t, at]

    phi = halves(phi_ref[...])

    @pl.loop(0, steps)
    def _(r):
        at = pl.ds(pl.multiple_of(r * rows, rows), rows)
        for t in range(trials):
            pair = dot3((high[t, at], low[t, at]), phi, ((1,), (0,))) * screened_ref[at]
            back_ref[t, at] += dot3(halves(pair), phi, ((1,), (1,)))


def tile(half_map, phi, screened, start, back):
    trials, points, orbitals = half_map.shape
    width = phi.shape[1]
    columns = math.gcd(math.gcd(width, start) if start else width, 512)
    rows = math.gcd(points, 256)
    offset = start // columns
    whole = pl.BlockSpec((trials, points, orbitals), lambda s: (0, 0, 0))
    specs = [
        whole,
        pl.BlockSpec((orbitals, columns), lambda s: (0, s)),
        pl.BlockSpec((points, columns), lambda s: (0, s + offset)),
    ]
    args = [half_map, phi, screened]
    if back is not None:
        specs.append(whole)
        args.append(back)
    return pl.pallas_call(
        functools.partial(tile_kernel, back is None, rows),
        grid=(width // columns,),
        out_shape=jax.ShapeDtypeStruct(half_map.shape, jnp.float32),
        in_specs=specs,
        out_specs=whole,
        scratch_shapes=[pltpu.VMEM(half_map.shape, jnp.bfloat16)] * 2,
        input_output_aliases={3: 0} if back is not None else {},
        cost_estimate=pl.CostEstimate(
            flops=12 * trials * points * orbitals * width,
            bytes_accessed=4 * (points * width + orbitals * width + 3 * trials * points * orbitals),
            transcendentals=0,
        ),
        name="tile",
    )(*args)


def local(n, m, x_trial, psi_orb, phi_orb, screened, eps_val, eps_cond):
    high = lax.Precision.HIGH
    width = phi_orb.shape[1]
    unit = width // sum(CHUNKS)
    phi_cols, start = [], 0
    for count in CHUNKS:
        piece = lax.slice_in_dim(phi_orb, start, start + count * unit, axis=1)
        phi_cols.append((start, lax.all_gather(piece, "wide", axis=0, tiled=True)))
        start += count * unit
    x_all, psi_all = spread(n, m, x_trial, psi_orb)
    trials, vals, conds = x_trial.shape
    psi_rows = psi_all.reshape(m * psi_orb.shape[0], psi_orb.shape[1])
    x_whole = jnp.transpose(x_all, (2, 1, 3, 0, 4)).reshape(trials, n * vals, m * conds)
    back = None
    half_map = jnp.einsum("vr,tvc->trc", psi_rows, x_whole, precision=high)
    for start, phi in phi_cols:
        back = tile(half_map, phi, screened, start, back)
    summed = lax.psum_scatter(back, "narrow", scatter_dimension=2, tiled=True)
    part = jnp.einsum("vr,trc->vtc", psi_rows, summed, precision=high)
    part = jnp.swapaxes(part.reshape(n, vals, trials, conds), 1, 2)
    kernel = collect(n, part)
    energy_gap = eps_cond[None, None, :] - eps_val[None, :, None]
    return kernel + energy_gap * x_trial


def solution(mesh):
    placed = (
        P(None, "wide", "narrow"),
        P("narrow", "wide"),
        P("wide", "narrow"),
        P("wide", "narrow"),
        P("wide"),
        P("narrow"),
    )
    return jax.shard_map(
        functools.partial(local, mesh.shape["wide"], mesh.shape["narrow"]),
        mesh=mesh, in_specs=placed, out_specs=P(None, "wide", "narrow"), check_vma=False,
    )
```

time: 647 us -> 461 us (0.71)
  Pallas kernels: 0 us -> 241 us
  matrix products: 244 us -> 12.2 us
  waiting for transfers between devices: 379 us -> 182 us
  local copies, waits for them, and re-layouts: 2.76 us -> 10.3 us
    pallas_call x0 -> x7, Pallas kernels: none -> 241 us  [the longest x5 164 us: tile(): pl.pallas_call(functools.partial(tile_kernel, back is None, rows), grid=(...]
    dot_general x4 -> x2, matrix products: 244 us -> 12.2 us  [the longest x1 7.8 us: local(): half_map = jnp.einsum('vr,tvc->trc', psi_rows, x_whole, precision=high)]
    unnamed x6, waiting for transfers between devices: 113 us -> 1.96 us
    all_gather x3 -> x5, waiting for transfers between devices: 253 us -> 168 us  [local(): phi_cols.append((start, lax.all_gather(piece, 'wide', axis=0, tiled=True)))]
  transfers between devices with their start and end apart: 5 -> 6, of which waited for: 5 -> 6; matrix products, arithmetic and copies ran while one was open for 2% -> 3% of each run, Pallas kernels for 0% -> 40%
where the time goes in v1:
time: 461 us
  Pallas kernels  241 us (52%)
  waiting for transfers between devices  182 us (39%)
  between operations  13.5 us (3%)
  matrix products  12.2 us (3%)
  local copies, waits for them, and re-layouts  10.3 us (2%)
    all_gather x5, waiting for transfers between devices, local(): phi_cols.append((start, lax.all_gather(piece, 'wide', axis=0, tiled=True)))  168 us
    pallas_call x5, Pallas kernels, tile(): pl.pallas_call(functools.partial(tile_kernel, back is None, rows), grid=(...  164 us
    pallas_call x1, Pallas kernels, spread(): pl.pallas_call(functools.partial(spread_kernel, n, m), out_shape=(jax.Sha...  42.6 us
    pallas_call x1, Pallas kernels, collect(): pl.pallas_call(functools.partial(collect_kernel, n), out_shape=jax.ShapeD...  34.6 us
    reduce_scatter x1, waiting for transfers between devices, local(): summed = lax.psum_scatter(back, 'narrow', scatter_dimension=2, tiled=True)  11.4 us
  transfers between devices with their start and end apart: 6, of which 6 were waited for; matrix products, arithmetic and copies ran while one was open for 3% of the time, Pallas kernels for 40%

profile of v1, /device:TPU:14, one launch (start us, length us, event | category | flops | bytes accessed | tf_op | source)
XLA Modules:
  0.0 460.6 jit_solution(4802175852759351499)
XLA Ops:
  6.5 2.0 fusion.5
  8.6 0.0 all-gather.14.cloned.1.call-update
  8.6 0.0 all-gather.12.cloned.1.call-start
  8.6 0.7 all-gather.12.cloned.1.call-update
  9.3 0.0 all-gather.10.cloned.1.call-start
  9.4 0.7 all-gather.10.cloned.1.call-update
  10.1 0.0 all-gather.8.cloned.1.call-start
  10.1 1.7 fusion.6
  11.8 0.0 all-gather.6.cloned.1.call-start
  11.9 0.5 all-gather.6.cloned.1.call-update
  12.4 0.0 reduce-scatter.2.cloned.1.call-start
  12.5 42.6 %spread.1 = (f32[2,16,2,32,256]{4,3,2,1,0:T(8,128)}, f32[2,256,1024]{2,1,0:T(8,128)}) custom-call(f32[2,32,256]{2,1,0:T(8,128)} %x_ref.1, f32[256,1024]{1,0:T(8,128)} %psi_ref.1), custom_call_target="tpu_custom_call" | custom-call | tf_op jit(solution)/shard_map/spread/pallas_call | solution.py:78
  55.1 3.3 copy.12
  58.4 2.7 reshape.41
  61.1 7.8 %convolution_bitcast_fusion.half_ref = f32[2,1024,512]{2,1,0:T(8,128)} fusion(f32[2,512,512]{2,1,0:T(8,128)} %reshape.41, f32[512,1024,1]{1,0,2:T(8,128)} %bitcast.21), kind=kOutput, calls=%fused_computation | convolution fusion | flops 3221225472 | bytes 8388608 | tf_op jit(solution)/shard_map/vr,tvc->trc/dot_general | solution.py:229
  68.9 31.4 %all-gather.14.cloned.1.call-done.phi_ref = f32[512,2048]{1,0:T(8,128)} async-done(((f32[32,2048]{1,0:T(8,128)}), f32[512,2048]{1,0:T(8,128)}) %all-gather.14.cloned.1.call-update) | async-done | bytes 4194320 | tf_op jit(solution)/shard_map/all_gather | solution.py:222
  100.2 38.6 %tile.5.refs_0_ = f32[2,1024,512]{2,1,0:T(8,128)} custom-call(f32[2,1024,512]{2,1,0:T(8,128)} %convolution_bitcast_fusion.half_ref, f32[512,2048]{1,0:T(8,128)} %all-gather.14.cloned.1.call-done.phi_ref, f32[1024,8192]{1,0:T(8,128)} %screened_ref.9), custom_call_target="tpu_custom_call" | custom-call | flops 25769803776 | bytes 25165824 | tf_op jit(solution)/shard_map/tile/pallas_call | solution.py:198
  138.9 38.4 %all-gather.12.cloned.1.call-done.phi_ref = f32[512,2048]{1,0:T(8,128)} async-done(((f32[32,2048]{1,0:T(8,128)}), f32[512,2048]{1,0:T(8,128)}) %all-gather.12.cloned.1.call-update) | async-done | bytes 4194320 | tf_op jit(solution)/shard_map/all_gather | solution.py:222
  177.3 39.4 %tile.6.refs_0_ = f32[2,1024,512]{2,1,0:T(8,128)} custom-call(f32[2,1024,512]{2,1,0:T(8,128)} %convolution_bitcast_fusion.half_ref, f32[512,2048]{1,0:T(8,128)} %all-gather.12.cloned.1.call-done.phi_ref, f32[1024,8192]{1,0:T(8,128)} %screened_ref.9, f32[2,1024,512]{2,1,0:T(8,128)} %tile.5.refs_0_), custom_call_target="tpu_custom_call", output_to_operand_aliasing={{}: (3, {})} | custom-call | flops 25769803776 | bytes 25165824 | tf_op jit(solution)/shard_map/tile/pallas_call | solution.py:198
  216.6 37.7 %all-gather.10.cloned.1.call-done.phi_ref = f32[512,2048]{1,0:T(8,128)} async-done(((f32[32,2048]{1,0:T(8,128)}), f32[512,2048]{1,0:T(8,128)}) %all-gather.10.cloned.1.call-update) | async-done | bytes 4194320 | tf_op jit(solution)/shard_map/all_gather | solution.py:222
  254.3 39.4 %tile.7.refs_0_ = f32[2,1024,512]{2,1,0:T(8,128)} custom-call(f32[2,1024,512]{2,1,0:T(8,128)} %convolution_bitcast_fusion.half_ref, f32[512,2048]{1,0:T(8,128)} %all-gather.10.cloned.1.call-done.phi_ref, f32[1024,8192]{1,0:T(8,128)} %screened_ref.9, f32[2,1024,512]{2,1,0:T(8,128)} %tile.6.refs_0_), custom_call_target="tpu_custom_call", output_to_operand_aliasing={{}: (3, {})} | custom-call | flops 25769803776 | bytes 25165824 | tf_op jit(solution)/shard_map/tile/pallas_call | solution.py:198
  293.7 22.3 %all-gather.8.cloned.1.call-done.phi_ref = f32[512,1024]{1,0:T(8,128)} async-done(((f32[32,1024]{1,0:T(8,128)}), f32[512,1024]{1,0:T(8,128)}) %all-gather.8.cloned.1.call-update) | async-done | bytes 2097168 | tf_op jit(solution)/shard_map/all_gather | solution.py:222
  316.0 23.2 %tile.8.refs_0_ = f32[2,1024,512]{2,1,0:T(8,128)} custom-call(f32[2,1024,512]{2,1,0:T(8,128)} %convolution_bitcast_fusion.half_ref, f32[512,1024]{1,0:T(8,128)} %all-gather.8.cloned.1.call-done.phi_ref, f32[1024,8192]{1,0:T(8,128)} %screened_ref.9, f32[2,1024,512]{2,1,0:T(8,128)} %tile.7.refs_0_), custom_call_target="tpu_custom_call", output_to_operand_aliasing={{}: (3, {})} | custom-call | flops 12884901888 | bytes 18874368 | tf_op jit(solution)/shard_map/tile/pallas_call | solution.py:198
  339.2 38.6 %all-gather.6.cloned.1.call-done.phi_ref = f32[512,1024]{1,0:T(8,128)} async-done(((f32[32,1024]{1,0:T(8,128)}), f32[512,1024]{1,0:T(8,128)}) %all-gather.6.cloned.1.call-update) | async-done | bytes 2097168 | tf_op jit(solution)/shard_map/all_gather | solution.py:222
  377.8 23.2 %tile.9 = f32[2,1024,512]{2,1,0:T(8,128)} custom-call(f32[2,1024,512]{2,1,0:T(8,128)} %convolution_bitcast_fusion.half_ref, f32[512,1024]{1,0:T(8,128)} %all-gather.6.cloned.1.call-done.phi_ref, f32[1024,8192]{1,0:T(8,128)} %screened_ref.9, f32[2,1024,512]{2,1,0:T(8,128)} %tile.8.refs_0_), custom_call_target="tpu_custom_call", output_to_operand_aliasing={{}: (3, {})} | custom-call | flops 12884901888 | bytes 18874368 | tf_op jit(solution)/shard_map/tile/pallas_call | solution.py:198
  401.1 0.0 reduce-scatter.2.cloned.1.call-update
  401.1 0.6 copy-done.2
  401.8 0.1 broadcast_subtract_fusion
  401.8 11.4 %reduce-scatter.2.cloned.1.call-done = f32[2,1024,256]{2,1,0:T(8,128)} async-done(((f32[2,1024,512]{2,1,0:T(8,128)}), f32[2,1024,256]{2,1,0:T(8,128)}) %reduce-scatter.2.cloned.1.call-update) | async-done | bytes 2097168 | tf_op jit(solution)/shard_map/reduce_scatter | solution.py:232
  413.2 4.4 fusion.2.part_ref
  417.7 34.6 %collect.1 = f32[2,32,256]{2,1,0:T(8,128)} custom-call(f32[16,2,32,256]{3,2,1,0:T(8,128)} %fusion.2.part_ref), custom_call_target="tpu_custom_call" | custom-call | tf_op jit(solution)/shard_map/collect/pallas_call | solution.py:128
  452.3 1.5 multiply_add_fusion
  (9 shorter events, 0.0 us)
Async XLA Ops:
  6.5 93.7 %all-gather.14.cloned.1.call-start = ((), (), s32[]{:S(2)}) async-start(), calls=%async_computation.5 | async-start | bytes 4456448 | tf_op jit(solution)/shard_map/all_gather | solution.py:222
  8.6 168.7 %all-gather.12.cloned.1.call-start = ((), (), s32[]{:S(2)}) async-start(), calls=%async_computation.4 | async-start | bytes 4456448 | tf_op jit(solution)/shard_map/all_gather | solution.py:222
  9.3 245.0 %all-gather.10.cloned.1.call-start = ((), (), s32[]{:S(2)}) async-start(), calls=%async_computation.3 | async-start | bytes 4456448 | tf_op jit(solution)/shard_map/all_gather | solution.py:222
  10.1 305.9 %all-gather.8.cloned.1.call-start = ((), (), s32[]{:S(2)}) async-start(), calls=%async_computation.2 | async-start | bytes 2228224 | tf_op jit(solution)/shard_map/all_gather | solution.py:222
  11.8 366.0 %all-gather.6.cloned.1.call-start = ((), (), s32[]{:S(2)}) async-start(), calls=%async_computation.1 | async-start | bytes 2228224 | tf_op jit(solution)/shard_map/all_gather | solution.py:222
  12.4 400.8 %reduce-scatter.2.cloned.1.call-start = ((), (), s32[]{:S(2)}) async-start(), calls=%async_computation.6 | async-start | bytes 6291456 | tf_op jit(solution)/shard_map/reduce_scatter | solution.py:232
  401.1 0.7 copy-start.2
  401.1 0.7 copy-start.3
  401.1 12.1 %copy-start = (f32[2,256,1024]{2,1,0:T(8,128)S(1)}, f32[2,256,1024]{2,1,0:T(8,128)}, u32[]{:S(2)}) copy-start(f32[2,256,1024]{2,1,0:T(8,128)} %get-tuple-element.7) | copy-start | bytes 6291460
  413.2 39.1 %copy-start.1 = (f32[2,32,256]{2,1,0:T(8,128)S(1)}, f32[2,32,256]{2,1,0:T(8,128)}, u32[]{:S(2)}) copy-start(f32[2,32,256]{2,1,0:T(8,128)} %x_ref.1) | copy-start | bytes 196612
Sparse Core Ops, SparseCore 0:
  10.1 90.0 all-gather.13
  103.0 74.2 all-gather.11
  180.0 74.2 all-gather.9
  256.9 59.0 all-gather.7
  318.6 59.1 all-gather.5
  401.2 11.9 reduce-scatter.1

commit v2 on v1

--- a/solution.py
+++ b/solution.py
@@ -10,7 +10,7 @@
 
 MESH = pl.DeviceIdType.MESH
 VM = pl.BlockSpec(memory_space=pltpu.VMEM)
-CHUNKS = (2, 2, 2, 1, 1)
+CHUNKS = (5, 3)
 
 
 def spread_kernel(n, m, x_ref, psi_ref, xs_ref, psis_ref, xs_sem, xr_sem, fs_sem, fr_sem, ps_sem, pr_sem, own_sem):

time: 461 us -> 369 us (0.80)
  waiting for transfers between devices: 182 us -> 102 us
  Pallas kernels: 241 us -> 229 us
    all_gather x5 -> x2, waiting for transfers between devices: 168 us -> 91 us  [local(): phi_cols.append((start, lax.all_gather(piece, 'wide', axis=0, tiled=True)))]
    pallas_call x5 -> x2, Pallas kernels: 164 us -> 143 us  [tile(): pl.pallas_call(functools.partial(tile_kernel, back is None, rows), grid=(...]
    pallas_call x1, Pallas kernels: 42.6 us -> 51.9 us  [spread(): pl.pallas_call(functools.partial(spread_kernel, n, m), out_shape=(jax.Sha...]
  transfers between devices with their start and end apart: 6 -> 3, of which waited for: 6 -> 3; matrix products, arithmetic and copies ran while one was open for 3% -> 4% of each run, Pallas kernels for 40% -> 38%
where the time goes in v2:
time: 369 us
  Pallas kernels  229 us (62%)
  waiting for transfers between devices  102 us (28%)
  between operations  13.1 us (4%)
  matrix products  12.2 us (3%)
  local copies, waits for them, and re-layouts  10.4 us (3%)
    pallas_call x2, Pallas kernels, tile(): pl.pallas_call(functools.partial(tile_kernel, back is None, rows), grid=(...  143 us
    all_gather x2, waiting for transfers between devices, local(): phi_cols.append((start, lax.all_gather(piece, 'wide', axis=0, tiled=True)))  91 us
    pallas_call x1, Pallas kernels, spread(): pl.pallas_call(functools.partial(spread_kernel, n, m), out_shape=(jax.Sha...  51.9 us
    pallas_call x1, Pallas kernels, collect(): pl.pallas_call(functools.partial(collect_kernel, n), out_shape=jax.ShapeD...  34.6 us
    reduce_scatter x1, waiting for transfers between devices, local(): summed = lax.psum_scatter(back, 'narrow', scatter_dimension=2, tiled=True)  11.4 us
    dot_general x1, matrix products, local(): half_map = jnp.einsum('vr,tvc->trc', psi_rows, x_whole, precision=high)  7.74 us
  transfers between devices with their start and end apart: 3, of which 3 were waited for; matrix products, arithmetic and copies ran while one was open for 4% of the time, Pallas kernels for 38%

profile of v2, /device:TPU:14, one launch (start us, length us, event | category | flops | bytes accessed | tf_op | source)
XLA Modules:
  0.0 368.9 jit_solution(15795257860168453863)
XLA Ops:
  6.5 0.0 all-gather.5.cloned.1.call-start
  6.5 2.0 slice.7
  8.5 0.0 all-gather.5.cloned.1.call-update
  8.5 0.0 all-gather.3.cloned.1.call-start
  8.6 1.8 slice.6
  10.4 0.0 all-gather.3.cloned.1.call-update
  10.4 0.0 reduce-scatter.2.cloned.1.call-start
  10.4 51.9 %spread.1 = (f32[2,16,2,32,256]{4,3,2,1,0:T(8,128)}, f32[2,256,1024]{2,1,0:T(8,128)}) custom-call(f32[2,32,256]{2,1,0:T(8,128)} %x_ref.1, f32[256,1024]{1,0:T(8,128)} %psi_ref.1), custom_call_target="tpu_custom_call" | custom-call | tf_op jit(solution)/shard_map/spread/pallas_call | solution.py:78
  62.4 3.3 copy.9
  65.6 2.7 reshape.41
  68.4 7.7 %convolution_bitcast_fusion.half_ref = f32[2,1024,512]{2,1,0:T(8,128)} fusion(f32[2,512,512]{2,1,0:T(8,128)} %reshape.41, f32[512,1024,1]{1,0,2:T(8,128)} %bitcast.21), kind=kOutput, calls=%fused_computation | convolution fusion | flops 3221225472 | bytes 8388608 | tf_op jit(solution)/shard_map/vr,tvc->trc/dot_general | solution.py:229
  76.1 82.5 %all-gather.5.cloned.1.call-done.phi_ref = f32[512,5120]{1,0:T(8,128)} async-done(((f32[32,5120]{1,0:T(8,128)}), f32[512,5120]{1,0:T(8,128)}) %all-gather.5.cloned.1.call-update) | async-done | bytes 10485776 | tf_op jit(solution)/shard_map/all_gather | solution.py:222
  158.6 87.1 %tile.2.refs_0_ = f32[2,1024,512]{2,1,0:T(8,128)} custom-call(f32[2,1024,512]{2,1,0:T(8,128)} %convolution_bitcast_fusion.half_ref, f32[512,5120]{1,0:T(8,128)} %all-gather.5.cloned.1.call-done.phi_ref, f32[1024,8192]{1,0:T(8,128)} %screened_ref.3), custom_call_target="tpu_custom_call" | custom-call | flops 64424509440 | bytes 44040192 | tf_op jit(solution)/shard_map/tile/pallas_call | solution.py:198
  245.7 8.5 %all-gather.3.cloned.1.call-done.phi_ref = f32[512,3072]{1,0:T(8,128)} async-done(((f32[32,3072]{1,0:T(8,128)}), f32[512,3072]{1,0:T(8,128)}) %all-gather.3.cloned.1.call-update) | async-done | bytes 6291472 | tf_op jit(solution)/shard_map/all_gather | solution.py:222
  254.1 55.6 %tile.3 = f32[2,1024,512]{2,1,0:T(8,128)} custom-call(f32[2,1024,512]{2,1,0:T(8,128)} %convolution_bitcast_fusion.half_ref, f32[512,3072]{1,0:T(8,128)} %all-gather.3.cloned.1.call-done.phi_ref, f32[1024,8192]{1,0:T(8,128)} %screened_ref.3, f32[2,1024,512]{2,1,0:T(8,128)} %tile.2.refs_0_), custom_call_target="tpu_custom_call", output_to_operand_aliasing={{}: (3, {})} | custom-call | flops 38654705664 | bytes 31457280 | tf_op jit(solution)/shard_map/tile/pallas_call | solution.py:198
  309.7 0.0 copy-start.2
  309.7 0.0 copy-start.3
  309.7 0.0 copy-start
  309.7 0.0 reduce-scatter.2.cloned.1.call-update
  309.7 0.6 copy-done.2
  310.4 0.0 copy-done.3
  310.4 0.1 broadcast_subtract_fusion
  310.5 11.4 %reduce-scatter.2.cloned.1.call-done = f32[2,1024,256]{2,1,0:T(8,128)} async-done(((f32[2,1024,512]{2,1,0:T(8,128)}), f32[2,1024,256]{2,1,0:T(8,128)}) %reduce-scatter.2.cloned.1.call-update) | async-done | bytes 2097168 | tf_op jit(solution)/shard_map/reduce_scatter | solution.py:232
  321.9 0.0 copy-done
  321.9 0.0 copy-start.1
  321.9 4.4 %fusion.2.part_ref = f32[16,2,32,256]{3,2,1,0:T(8,128)} fusion(f32[16,32,1024,1]{2,1,3,0:T(8,128)S(1)} %bitcast.22, f32[2,1024,256]{2,1,0:T(8,128)} %reduce-scatter.2.cloned.1.call-done), kind=kOutput, calls=%fused_computation.3 | convolution fusion | flops 1610612736 | bytes 5242880 | tf_op jit(solution)/shard_map/vr,trc->vtc/dot_general | solution.py:233
  326.3 34.6 %collect.1 = f32[2,32,256]{2,1,0:T(8,128)} custom-call(f32[16,2,32,256]{3,2,1,0:T(8,128)} %fusion.2.part_ref), custom_call_target="tpu_custom_call" | custom-call | tf_op jit(solution)/shard_map/collect/pallas_call | solution.py:128
  360.9 0.0 copy-done.1
  360.9 1.5 multiply_add_fusion
Async XLA Ops:
  6.5 152.1 %all-gather.5.cloned.1.call-start = ((), (), s32[]{:S(2)}) async-start(), calls=%async_computation.2 | async-start | bytes 11141120 | tf_op jit(solution)/shard_map/all_gather | solution.py:222
  8.5 245.6 %all-gather.3.cloned.1.call-start = ((), (), s32[]{:S(2)}) async-start(), calls=%async_computation.1 | async-start | bytes 6684672 | tf_op jit(solution)/shard_map/all_gather | solution.py:222
  10.4 311.5 %reduce-scatter.2.cloned.1.call-start = ((), (), s32[]{:S(2)}) async-start(), calls=%async_computation.3 | async-start | bytes 6291456 | tf_op jit(solution)/shard_map/reduce_scatter | solution.py:232
  309.7 0.7 copy-start.2
  309.7 0.7 copy-start.3
  309.7 12.2 %copy-start = (f32[2,256,1024]{2,1,0:T(8,128)S(1)}, f32[2,256,1024]{2,1,0:T(8,128)}, u32[]{:S(2)}) copy-start(f32[2,256,1024]{2,1,0:T(8,128)} %get-tuple-element.7) | copy-start | bytes 6291460
  321.9 39.0 %copy-start.1 = (f32[2,32,256]{2,1,0:T(8,128)S(1)}, f32[2,32,256]{2,1,0:T(8,128)}, u32[]{:S(2)}) copy-start(f32[2,32,256]{2,1,0:T(8,128)} %x_ref.1) | copy-start | bytes 196612
Sparse Core Ops, SparseCore 0:
  10.0 148.5 all-gather.4
  161.4 92.7 all-gather.2
  309.9 11.9 reduce-scatter.1

commit v3 on v2

--- a/solution.py
+++ b/solution.py
@@ -10,12 +10,26 @@
 
 MESH = pl.DeviceIdType.MESH
 VM = pl.BlockSpec(memory_space=pltpu.VMEM)
-CHUNKS = (5, 3)
-
-
-def spread_kernel(n, m, x_ref, psi_ref, xs_ref, psis_ref, xs_sem, xr_sem, fs_sem, fr_sem, ps_sem, pr_sem, own_sem):
+CHUNKS = (4, 4)
+PIECES = 4
+
+
+def spread_kernel(dims, m, x_ref, psi_ref, phi_ref, xs_ref, psis_ref, phis_ref, xs_sem, xr_sem, fs_sem, fr_sem,
+                  ps_sem, pr_sem, own_sem, gs_sem, gr_sem):
+    zs, ys, xs = dims
+    n = zs * ys * xs
     w = lax.axis_index("wide")
     c = lax.axis_index("narrow")
+    spot = (w // (ys * xs), lax.rem(w // xs, ys), lax.rem(w, xs))
+    columns = phi_ref.shape[1] // PIECES
+
+    def moved(at, axis, by):
+        at = list(at)
+        at[axis] = lax.rem(at[axis] + by, dims[axis])
+        return tuple(at)
+
+    def flat(at):
+        return (at[0] * ys + at[1]) * xs + at[2]
 
     def psi_copy(slot, peer, k):
         return pltpu.make_async_remote_copy(
@@ -31,6 +45,36 @@
         return pltpu.make_async_remote_copy(
             src_ref=src, dst_ref=xs_ref.at[slot_c, slot], send_sem=fs_sem.at[k, slot],
             recv_sem=fr_sem.at[slot_c, slot], device_id=(w, peer), device_id_type=MESH)
+
+    def phi_copy(piece, block, peer, k, own=False):
+        at = pl.ds(piece * columns, columns)
+        held = phis_ref.at[block, :, at]
+        return pltpu.make_async_remote_copy(
+            src_ref=phi_ref.at[:, at] if own else held, dst_ref=held, send_sem=gs_sem.at[piece, k],
+            recv_sem=gr_sem.at[piece, block], device_id=(peer, c), device_id_type=MESH)
+
+    sent = [[] for _ in range(PIECES)]
+
+    def phi_send(piece, block, axes, own=False):
+        for axis in axes:
+            for by in range(1, dims[axis]):
+                copy = phi_copy(piece, block, flat(moved(spot, axis, by)), len(sent[piece]), own)
+                copy.start()
+                sent[piece].append(copy)
+
+    def order(piece):
+        return (0, 1, 2) if piece % 2 == 0 else (0, 2, 1)
+
+    def arrivals(piece, stage):
+        axes = order(piece)
+        found = [spot]
+        for axis in axes[:stage]:
+            found = [moved(at, axis, by) for at in found for by in range(dims[axis])]
+        axis = axes[stage]
+        return [flat(moved(at, axis, dims[axis] - by)) for by in range(1, dims[axis]) for at in found]
+
+    for piece in range(PIECES):
+        phi_send(piece, w, order(piece), own=True)
 
     @pl.loop(1, n)
     def _(i):
@@ -43,8 +87,18 @@
 
     own_x = pltpu.make_async_copy(x_ref, xs_ref.at[c, w], own_sem.at[0])
     own_psi = pltpu.make_async_copy(psi_ref, psis_ref.at[c], own_sem.at[1])
+    own_phi = pltpu.make_async_copy(phi_ref, phis_ref.at[w], own_sem.at[2])
     own_x.start()
     own_psi.start()
+    own_phi.start()
+
+    for step in range(PIECES + 1):
+        for stage in (1, 0):
+            piece = step - stage
+            if 0 <= piece < PIECES:
+                for block in arrivals(piece, stage):
+                    phi_copy(piece, block, w, 0).wait_recv()
+                    phi_send(piece, block, order(piece)[stage + 1:])
 
     @pl.loop(1, n)
     def _(i):
@@ -57,6 +111,7 @@
 
     own_x.wait()
     own_psi.wait()
+    own_phi.wait()
 
     @pl.loop(1, m)
     def _(j):
@@ -73,16 +128,24 @@
     def _(i):
         x_copy(w, w, i).wait_send()
 
-
-def spread(n, m, x_trial, psi_orb):
+    for piece in range(PIECES):
+        for block in arrivals(piece, 2):
+            phi_copy(piece, block, w, 0).wait_recv()
+        for copy in sent[piece]:
+            copy.wait_send()
+
+
+def spread(dims, m, x_trial, psi_orb, phi_piece):
+    n = math.prod(dims)
     return pl.pallas_call(
-        functools.partial(spread_kernel, n, m),
+        functools.partial(spread_kernel, dims, m),
         out_shape=(
             jax.ShapeDtypeStruct((m, n) + x_trial.shape, jnp.float32),
             jax.ShapeDtypeStruct((m,) + psi_orb.shape, jnp.float32),
+            jax.ShapeDtypeStruct((n,) + phi_piece.shape, jnp.float32),
         ),
-        in_specs=[VM, VM],
-        out_specs=(VM, VM),
+        in_specs=[VM, VM, VM],
+        out_specs=(VM, VM, pl.BlockSpec(memory_space=pl.ANY)),
         scratch_shapes=[
             pltpu.SemaphoreType.DMA((n,)),
             pltpu.SemaphoreType.DMA((n,)),
@@ -90,11 +153,13 @@
             pltpu.SemaphoreType.DMA((m, n)),
             pltpu.SemaphoreType.DMA((m,)),
             pltpu.SemaphoreType.DMA((m,)),
-            pltpu.SemaphoreType.DMA((2,)),
+            pltpu.SemaphoreType.DMA((3,)),
+            pltpu.SemaphoreType.DMA((PIECES, n)),
+            pltpu.SemaphoreType.DMA((PIECES, n)),
         ],
         compiler_params=pltpu.CompilerParams(has_side_effects=True),
         name="spread",
-    )(x_trial, psi_orb)
+    )(x_trial, psi_orb, phi_piece)
 
 
 def collect_kernel(n, part_ref, out_ref, got, s_sem, r_sem):
@@ -212,16 +277,14 @@
     )(*args)
 
 
-def local(n, m, x_trial, psi_orb, phi_orb, screened, eps_val, eps_cond):
+def local(dims, m, x_trial, psi_orb, phi_orb, screened, eps_val, eps_cond):
     high = lax.Precision.HIGH
-    width = phi_orb.shape[1]
-    unit = width // sum(CHUNKS)
-    phi_cols, start = [], 0
-    for count in CHUNKS:
-        piece = lax.slice_in_dim(phi_orb, start, start + count * unit, axis=1)
-        phi_cols.append((start, lax.all_gather(piece, "wide", axis=0, tiled=True)))
-        start += count * unit
-    x_all, psi_all = spread(n, m, x_trial, psi_orb)
+    n = math.prod(dims)
+    orbitals, width = phi_orb.shape
+    cut = width * CHUNKS[0] // sum(CHUNKS)
+    late = lax.all_gather(lax.slice_in_dim(phi_orb, cut, width, axis=1), "wide", axis=0, tiled=True)
+    x_all, psi_all, early = spread(dims, m, x_trial, psi_orb, lax.slice_in_dim(phi_orb, 0, cut, axis=1))
+    phi_cols = ((0, early.reshape(n * orbitals, cut)), (cut, late))
     trials, vals, conds = x_trial.shape
     psi_rows = psi_all.reshape(m * psi_orb.shape[0], psi_orb.shape[1])
     x_whole = jnp.transpose(x_all, (2, 1, 3, 0, 4)).reshape(trials, n * vals, m * conds)
@@ -237,6 +300,15 @@
     return kernel + energy_gap * x_trial
 
 
+def grid_of(mesh):
+    n = mesh.shape["wide"]
+    places = [getattr(d, "coords", None) for d in mesh.devices.reshape(n, -1)[:, 0]]
+    if None in places:
+        return 1, 1, n
+    xs, ys = (len({p[axis] for p in places}) for axis in (0, 1))
+    return (n // (xs * ys), ys, xs) if n % (xs * ys) == 0 else (1, 1, n)
+
+
 def solution(mesh):
     placed = (
         P(None, "wide", "narrow"),
@@ -247,6 +319,6 @@
         P("narrow"),
     )
     return jax.shard_map(
-        functools.partial(local, mesh.shape["wide"], mesh.shape["narrow"]),
+        functools.partial(local, grid_of(mesh), mesh.shape["narrow"]),
         mesh=mesh, in_specs=placed, out_specs=P(None, "wide", "narrow"), check_vma=False,
     )

time: 369 us -> 370 us (level)
  Pallas kernels: 229 us -> 323 us
  waiting for transfers between devices: 102 us -> 10.8 us
    pallas_call x1, Pallas kernels: 51.9 us -> 146 us  [spread(): pl.pallas_call(functools.partial(spread_kernel, dims, m), out_shape=(jax....]
    all_gather x2 -> x1, waiting for transfers between devices: 91 us -> 0.01 us  [local(): lax.all_gather(lax.slice_in_dim(phi_orb, cut, width, axis=1), 'wide', axi...]
  transfers between devices with their start and end apart: 3 -> 2, of which waited for: 3 -> 1; matrix products, arithmetic and copies ran while one was open for 4% -> 4% of each run, Pallas kernels for 38% -> 59%
where the time goes in v3:
time: 370 us
  Pallas kernels  323 us (87%)
  between operations  13.4 us (4%)
  matrix products  12.1 us (3%)
  waiting for transfers between devices  10.8 us (3%)
  local copies, waits for them, and re-layouts  8.89 us (2%)
    pallas_call x1, Pallas kernels, spread(): pl.pallas_call(functools.partial(spread_kernel, dims, m), out_shape=(jax....  146 us
    pallas_call x2, Pallas kernels, tile(): pl.pallas_call(functools.partial(tile_kernel, back is None, rows), grid=(...  143 us
    pallas_call x1, Pallas kernels, collect(): pl.pallas_call(functools.partial(collect_kernel, n), out_shape=jax.ShapeD...  34.6 us
    reduce_scatter x1, waiting for transfers between devices, local(): summed = lax.psum_scatter(back, 'narrow', scatter_dimension=2, tiled=True)  10.7 us
    dot_general x1, matrix products, local(): half_map = jnp.einsum('vr,tvc->trc', psi_rows, x_whole, precision=high)  7.7 us
  transfers between devices with their start and end apart: 2, of which 1 were waited for; matrix products, arithmetic and copies ran while one was open for 4% of the time, Pallas kernels for 59%

profile of v3, /device:TPU:14, one launch (start us, length us, event | category | flops | bytes accessed | tf_op | source)
XLA Modules:
  0.0 369.9 jit_solution(15935697208079493748)
XLA Ops:
  6.5 0.0 all-gather.2.cloned.1.call-start
  6.5 2.2 fusion.5
  8.8 0.0 all-gather.2.cloned.1.call-update
  8.8 0.0 reduce-scatter.2.cloned.1.call-start
  8.9 145.8 %spread.1 = (f32[2,16,2,32,256]{4,3,2,1,0:T(8,128)}, f32[2,256,1024]{2,1,0:T(8,128)}, f32[16,32,4096]{2,1,0:T(8,128)}) custom-call(f32[2,32,256]{2,1,0:T(8,128)} %x_ref.1, f32[256,1024]{1,0:T(8,128)} %psi_ref.1, f32[32,4096]{1,0:T(8,128)} %get-tuple-element.12.phi_ref), custom_call_target="tpu_custom_call" | custom-call | tf_op jit(solution)/shard_map/spread/pallas_call | solution.py:140
  154.7 3.3 copy.9
  158.0 2.7 reshape.44
  160.7 7.7 %convolution_bitcast_fusion.half_ref = f32[2,1024,512]{2,1,0:T(8,128)} fusion(f32[2,512,512]{2,1,0:T(8,128)} %reshape.44, f32[512,1024,1]{1,0,2:T(8,128)} %bitcast.22), kind=kOutput, calls=%fused_computation | convolution fusion | flops 3221225472 | bytes 8388608 | tf_op jit(solution)/shard_map/vr,tvc->trc/dot_general | solution.py:292
  168.4 71.0 %tile.2.refs_0_ = f32[2,1024,512]{2,1,0:T(8,128)} custom-call(f32[2,1024,512]{2,1,0:T(8,128)} %convolution_bitcast_fusion.half_ref, f32[512,4096]{1,0:T(8,128)} %bitcast.25, f32[1024,8192]{1,0:T(8,128)} %screened_ref.3), custom_call_target="tpu_custom_call" | custom-call | flops 51539607552 | bytes 37748736 | tf_op jit(solution)/shard_map/tile/pallas_call | solution.py:263
  239.3 0.0 all-gather.2.cloned.1.call-done.phi_ref
  239.3 71.7 %tile.3 = f32[2,1024,512]{2,1,0:T(8,128)} custom-call(f32[2,1024,512]{2,1,0:T(8,128)} %convolution_bitcast_fusion.half_ref, f32[512,4096]{1,0:T(8,128)} %all-gather.2.cloned.1.call-done.phi_ref, f32[1024,8192]{1,0:T(8,128)} %screened_ref.3, f32[2,1024,512]{2,1,0:T(8,128)} %tile.2.refs_0_), custom_call_target="tpu_custom_call", output_to_operand_aliasing={{}: (3, {})} | custom-call | flops 51539607552 | bytes 37748736 | tf_op jit(solution)/shard_map/tile/pallas_call | solution.py:263
  311.1 0.0 copy-start.2
  311.1 0.0 copy-start.3
  311.1 0.0 copy-start
  311.1 0.0 reduce-scatter.2.cloned.1.call-update
  311.1 0.6 copy-done.2
  311.7 0.0 copy-done.3
  311.7 0.1 broadcast_subtract_fusion
  311.8 10.7 %reduce-scatter.2.cloned.1.call-done = f32[2,1024,256]{2,1,0:T(8,128)} async-done(((f32[2,1024,512]{2,1,0:T(8,128)}), f32[2,1024,256]{2,1,0:T(8,128)}) %reduce-scatter.2.cloned.1.call-update) | async-done | bytes 2097168 | tf_op jit(solution)/shard_map/reduce_scatter | solution.py:295
  322.5 0.0 copy-done
  322.5 0.0 copy-start.1
  322.5 4.4 %fusion.2.part_ref = f32[16,2,32,256]{3,2,1,0:T(8,128)} fusion(f32[16,32,1024,1]{2,1,3,0:T(8,128)S(1)} %bitcast.23, f32[2,1024,256]{2,1,0:T(8,128)} %reduce-scatter.2.cloned.1.call-done), kind=kOutput, calls=%fused_computation.3 | convolution fusion | flops 1610612736 | bytes 5242880 | tf_op jit(solution)/shard_map/vr,trc->vtc/dot_general | solution.py:296
  327.0 34.6 %collect.1 = f32[2,32,256]{2,1,0:T(8,128)} custom-call(f32[16,2,32,256]{3,2,1,0:T(8,128)} %fusion.2.part_ref), custom_call_target="tpu_custom_call" | custom-call | tf_op jit(solution)/shard_map/collect/pallas_call | solution.py:193
  361.6 0.0 copy-done.1
  361.6 1.5 multiply_add_fusion
Async XLA Ops:
  6.5 232.8 %all-gather.2.cloned.1.call-start = ((), (), s32[]{:S(2)}) async-start(), calls=%async_computation.1 | async-start | bytes 8912896 | tf_op jit(solution)/shard_map/all_gather | solution.py:285
  8.8 313.7 %reduce-scatter.2.cloned.1.call-start = ((), (), s32[]{:S(2)}) async-start(), calls=%async_computation.2 | async-start | bytes 6291456 | tf_op jit(solution)/shard_map/reduce_scatter | solution.py:295
  311.1 0.7 copy-start.2
  311.1 0.7 copy-start.3
  311.1 11.5 %copy-start = (f32[2,256,1024]{2,1,0:T(8,128)S(1)}, f32[2,256,1024]{2,1,0:T(8,128)}, u32[]{:S(2)}) copy-start(f32[2,256,1024]{2,1,0:T(8,128)} %get-tuple-element.8) | copy-start | bytes 6291460
  322.5 39.0 %copy-start.1 = (f32[2,32,256]{2,1,0:T(8,128)S(1)}, f32[2,32,256]{2,1,0:T(8,128)}, u32[]{:S(2)}) copy-start(f32[2,32,256]{2,1,0:T(8,128)} %x_ref.1) | copy-start | bytes 196612
Sparse Core Ops, SparseCore 0:
  10.1 165.8 all-gather.1
  311.2 11.2 reduce-scatter.1

commit v4 on v3

--- a/solution.py
+++ b/solution.py
@@ -10,8 +10,11 @@
 
 MESH = pl.DeviceIdType.MESH
 VM = pl.BlockSpec(memory_space=pltpu.VMEM)
-CHUNKS = (4, 4)
-PIECES = 4
+CHUNKS = (3, 5)
+PIECES = 6
+ROWS = 1024
+COLUMNS = 512
+UNROLL = 1
 
 
 def spread_kernel(dims, m, x_ref, psi_ref, phi_ref, xs_ref, psis_ref, phis_ref, xs_sem, xr_sem, fs_sem, fr_sem,
@@ -236,7 +239,7 @@
 
     phi = halves(phi_ref[...])
 
-    @pl.loop(0, steps)
+    @pl.loop(0, steps, unroll=UNROLL)
     def _(r):
         at = pl.ds(pl.multiple_of(r * rows, rows), rows)
         for t in range(trials):
@@ -247,8 +250,8 @@
 def tile(half_map, phi, screened, start, back):
     trials, points, orbitals = half_map.shape
     width = phi.shape[1]
-    columns = math.gcd(math.gcd(width, start) if start else width, 512)
-    rows = math.gcd(points, 256)
+    columns = math.gcd(math.gcd(width, start) if start else width, COLUMNS)
+    rows = math.gcd(points, ROWS)
     offset = start // columns
     whole = pl.BlockSpec((trials, points, orbitals), lambda s: (0, 0, 0))
     specs = [

time: 370 us -> 321 us (0.87)
  Pallas kernels: 323 us -> 266 us
  waiting for transfers between devices: 10.8 us -> 16.5 us
    pallas_call x1, Pallas kernels: 146 us -> 111 us  [spread(): pl.pallas_call(functools.partial(spread_kernel, dims, m), out_shape=(jax....]
    pallas_call x2, Pallas kernels: 143 us -> 120 us  [tile(): pl.pallas_call(functools.partial(tile_kernel, back is None, rows), grid=(...]
    all_gather x1, waiting for transfers between devices: 0.01 us -> 4.27 us  [local(): lax.all_gather(lax.slice_in_dim(phi_orb, cut, width, axis=1), 'wide', axi...]
  transfers between devices with their start and end apart: 2 -> 2, of which waited for: 1 -> 2; matrix products, arithmetic and copies ran while one was open for 4% -> 5% of each run, Pallas kernels for 59% -> 49%
where the time goes in v4:
time: 321 us
  Pallas kernels  266 us (83%)
  waiting for transfers between devices  16.5 us (5%)
  between operations  13.4 us (4%)
  matrix products  12.6 us (4%)
  local copies, waits for them, and re-layouts  10.4 us (3%)
    pallas_call x2, Pallas kernels, tile(): pl.pallas_call(functools.partial(tile_kernel, back is None, rows), grid=(...  120 us
    pallas_call x1, Pallas kernels, spread(): pl.pallas_call(functools.partial(spread_kernel, dims, m), out_shape=(jax....  111 us
    pallas_call x1, Pallas kernels, collect(): pl.pallas_call(functools.partial(collect_kernel, n), out_shape=jax.ShapeD...  34.6 us
    reduce_scatter x1, waiting for transfers between devices, local(): summed = lax.psum_scatter(back, 'narrow', scatter_dimension=2, tiled=True)  12.2 us
    dot_general x1, matrix products, local(): half_map = jnp.einsum('vr,tvc->trc', psi_rows, x_whole, precision=high)  8.12 us
  transfers between devices with their start and end apart: 2, of which 2 were waited for; matrix products, arithmetic and copies ran while one was open for 5% of the time, Pallas kernels for 49%

profile of v4, /device:TPU:14, one launch (start us, length us, event | category | flops | bytes accessed | tf_op | source)
XLA Modules:
  0.0 320.7 jit_solution(5645756216180311897)
XLA Ops:
  6.5 0.0 all-gather.2.cloned.1.call-start
  6.5 2.0 slice.7
  8.5 0.0 all-gather.2.cloned.1.call-update
  8.5 0.0 reduce-scatter.2.cloned.1.call-start
  8.6 1.8 slice.6.phi_ref
  10.4 111.2 %spread.1 = (f32[2,16,2,32,256]{4,3,2,1,0:T(8,128)}, f32[2,256,1024]{2,1,0:T(8,128)}, f32[16,32,3072]{2,1,0:T(8,128)}) custom-call(f32[2,32,256]{2,1,0:T(8,128)} %x_ref.1, f32[256,1024]{1,0:T(8,128)} %psi_ref.1, f32[32,3072]{1,0:T(8,128)} %slice.6.phi_ref), custom_call_target="tpu_custom_call" | custom-call | tf_op jit(solution)/shard_map/spread/pallas_call | solution.py:143
  121.6 3.3 %copy.9 = f32[2,16,32,2,256]{4,3,2,1,0:T(2,128)S(1)} copy(f32[2,16,32,2,256]{4,2,0,1,3:T(8,128)} %bitcast.24) | data formatting | bytes 4194304 | tf_op jit(solution)/shard_map/transpose | solution.py:293
  124.9 2.7 reshape.44
  127.6 8.1 %convolution_bitcast_fusion.half_ref = f32[2,1024,512]{2,1,0:T(8,128)} fusion(f32[2,512,512]{2,1,0:T(8,128)} %reshape.44, f32[512,1024,1]{1,0,2:T(8,128)} %bitcast.22), kind=kOutput, calls=%fused_computation | convolution fusion | flops 3221225472 | bytes 8388608 | tf_op jit(solution)/shard_map/vr,tvc->trc/dot_general | solution.py:295
  135.7 46.4 %tile.2.refs_0_ = f32[2,1024,512]{2,1,0:T(8,128)} custom-call(f32[2,1024,512]{2,1,0:T(8,128)} %convolution_bitcast_fusion.half_ref, f32[512,3072]{1,0:T(8,128)} %bitcast.25, f32[1024,8192]{1,0:T(8,128)} %screened_ref.3), custom_call_target="tpu_custom_call" | custom-call | flops 38654705664 | bytes 31457280 | tf_op jit(solution)/shard_map/tile/pallas_call | solution.py:266
  182.2 4.3 %all-gather.2.cloned.1.call-done.phi_ref = f32[512,5120]{1,0:T(8,128)} async-done(((f32[32,5120]{1,0:T(8,128)}), f32[512,5120]{1,0:T(8,128)}) %all-gather.2.cloned.1.call-update) | async-done | bytes 10485776 | tf_op jit(solution)/shard_map/all_gather | solution.py:288
  186.4 74.0 %tile.3 = f32[2,1024,512]{2,1,0:T(8,128)} custom-call(f32[2,1024,512]{2,1,0:T(8,128)} %convolution_bitcast_fusion.half_ref, f32[512,5120]{1,0:T(8,128)} %all-gather.2.cloned.1.call-done.phi_ref, f32[1024,8192]{1,0:T(8,128)} %screened_ref.3, f32[2,1024,512]{2,1,0:T(8,128)} %tile.2.refs_0_), custom_call_target="tpu_custom_call", output_to_operand_aliasing={{}: (3, {})} | custom-call | flops 64424509440 | bytes 44040192 | tf_op jit(solution)/shard_map/tile/pallas_call | solution.py:266
  260.5 0.0 copy-start.2
  260.5 0.0 copy-start.3
  260.5 0.0 copy-start
  260.5 0.0 reduce-scatter.2.cloned.1.call-update
  260.5 0.6 copy-done.2
  261.1 0.0 copy-done.3
  261.1 0.1 broadcast_subtract_fusion
  261.2 12.2 %reduce-scatter.2.cloned.1.call-done = f32[2,1024,256]{2,1,0:T(8,128)} async-done(((f32[2,1024,512]{2,1,0:T(8,128)}), f32[2,1024,256]{2,1,0:T(8,128)}) %reduce-scatter.2.cloned.1.call-update) | async-done | bytes 2097168 | tf_op jit(solution)/shard_map/reduce_scatter | solution.py:298
  273.4 0.0 copy-done
  273.4 0.0 copy-start.1
  273.4 4.4 %fusion.2.part_ref = f32[16,2,32,256]{3,2,1,0:T(8,128)} fusion(f32[16,32,1024,1]{2,1,3,0:T(8,128)S(1)} %bitcast.23, f32[2,1024,256]{2,1,0:T(8,128)} %reduce-scatter.2.cloned.1.call-done), kind=kOutput, calls=%fused_computation.3 | convolution fusion | flops 1610612736 | bytes 5242880 | tf_op jit(solution)/shard_map/vr,trc->vtc/dot_general | solution.py:299
  277.8 34.6 %collect.1 = f32[2,32,256]{2,1,0:T(8,128)} custom-call(f32[16,2,32,256]{3,2,1,0:T(8,128)} %fusion.2.part_ref), custom_call_target="tpu_custom_call" | custom-call | tf_op jit(solution)/shard_map/collect/pallas_call | solution.py:196
  312.4 0.0 copy-done.1
  312.4 1.5 multiply_add_fusion
Async XLA Ops:
  6.5 179.9 %all-gather.2.cloned.1.call-start = ((), (), s32[]{:S(2)}) async-start(), calls=%async_computation.1 | async-start | bytes 11141120 | tf_op jit(solution)/shard_map/all_gather | solution.py:288
  8.5 264.8 %reduce-scatter.2.cloned.1.call-start = ((), (), s32[]{:S(2)}) async-start(), calls=%async_computation.2 | async-start | bytes 6291456 | tf_op jit(solution)/shard_map/reduce_scatter | solution.py:298
  260.5 0.7 copy-start.2
  260.5 0.7 copy-start.3
  260.5 12.9 %copy-start = (f32[2,256,1024]{2,1,0:T(8,128)S(1)}, f32[2,256,1024]{2,1,0:T(8,128)}, u32[]{:S(2)}) copy-start(f32[2,256,1024]{2,1,0:T(8,128)} %get-tuple-element.8) | copy-start | bytes 6291460
  273.4 39.0 %copy-start.1 = (f32[2,32,256]{2,1,0:T(8,128)S(1)}, f32[2,32,256]{2,1,0:T(8,128)}, u32[]{:S(2)}) copy-start(f32[2,32,256]{2,1,0:T(8,128)} %x_ref.1) | copy-start | bytes 196612
Sparse Core Ops, SparseCore 0:
  10.0 176.3 all-gather.1
  260.6 12.7 reduce-scatter.1
